TPU v7x, 128 devices: a whole 4x4x4 slice. The times are simulated.
128 devices in a mesh: row: 8 (over z, core), col: 16 (over x, y).
Axes of the slice: x: 4, y: 4, z: 4, core: 2. Of those that a mesh axis runs over, the one named last changes fastest.
Arguments:
- normed: bfloat16 [8192, 7168], P(None, 'col'), may hold values from -44 to 44
- projection_weight: bfloat16 [7168, 3, 7168], P('col', None, 'row')
- adapter_down_weight: bfloat16 [7168, 16, 32], P(None, 'col'), may hold values from -0.0625 to 0.0625
- adapter_up_weight: bfloat16 [16, 2, 16, 7168], P(None, None, None, 'row'), may hold values from -0.47851562 to 0.47851562
- packed_prompt_length: int32 [64], replicated, may hold values from 64 to 512, as said below
- prompt_adapter_ids: int32 [64], replicated, may hold values from 0 to 63, as said below
- slot_adapter_ids: int32 [16], replicated, may hold values from 0 to 63, as said below
- prompt_page_slots: int32 [64, 4], replicated, may hold values from -1 to 159, as said below
Outputs:
- attended: bfloat16 [8192, 7168], P('col', 'row')
- kv_cache: bfloat16 [160, 128, 2, 7168], P('col', None, None, 'row')
Inputs may be any that keep to these rules, and one draw needn't show every extreme that they name: `packed_prompt_length`: the 64 lengths sum to 8192; one of them is exactly 512 and one exactly 64. `slot_adapter_ids`: distinct adapter ids. `prompt_adapter_ids`: every entry is one of slot_adapter_ids, and every loaded adapter is named by at least one prompt. `prompt_page_slots`: entry [i, j] is -1 where 128 * j >= packed_prompt_length[i]; otherwise it lies among slots 10 * c to 10 * c + 9, where c is the block of 512 packed tokens that holds the page's last token. No slot is named twice.
All inputs are finite; a program needn't handle non-finite values.
Results may differ from a plain program's by a relative error of at most 0.0072.
Values may be sent and summed in bfloat16 or wider, within the bound.
A program may use at most 256 MiB of HBM per device.

v0:
```python
import jax
import jax.numpy as jnp
from jax import lax
from jax.sharding import PartitionSpec as P

HEAD_DIM = 128
PAGE = 128
NEAR = 1
SLOTS_DEV = 10
adapter_scale = 2.0
masked_score = -1e30


def shifted(block, axis, distance):
    devices = range(lax.axis_size(axis))
    route = [(i - distance, i) for i in devices if i - distance in devices]
    return lax.ppermute(block, axis, route)


def start_table(packed_prompt_length):
    prompt_ends = jnp.cumsum(packed_prompt_length)
    return prompt_ends - packed_prompt_length


def slot_table(prompt_adapter_ids, slot_adapter_ids):
    active_slots = slot_adapter_ids.shape[0]
    matched = slot_adapter_ids[None, :] == prompt_adapter_ids[:, None]
    return jnp.sum(
        jnp.where(matched, jnp.arange(active_slots, dtype=jnp.int32)[None, :], 0), axis=1
    )


def token_prompts(positions, prompt_starts):
    inside = (positions[:, None] >= prompt_starts[None, :]).astype(jnp.int32)
    return jnp.sum(inside, axis=1) - 1


def token_slots(prompts, slot_of):
    prompt_count = slot_of.shape[0]
    onehot = prompts[:, None] == jnp.arange(prompt_count, dtype=jnp.int32)[None, :]
    return jnp.sum(jnp.where(onehot, slot_of[None, :], 0), axis=1)


def down_term(row_block, slots_here, down_cols, active_slots):
    combined_output = jnp.dot(row_block, down_cols, preferred_element_type=jnp.float32)
    combined_output = combined_output.reshape(row_block.shape[0], active_slots, -1)
    pick_slot = slots_here[:, None] == jnp.arange(active_slots, dtype=jnp.int32)[None, :]
    return jnp.sum(jnp.where(pick_slot[:, :, None], combined_output, 0.0), axis=1)


def local(
    normed,
    projection_weight,
    adapter_down_weight,
    adapter_up_weight,
    packed_prompt_length,
    prompt_adapter_ids,
    slot_adapter_ids,
    prompt_page_slots,
):
    col_count = lax.axis_size("col")
    row_count = lax.axis_size("row")
    col_index = lax.axis_index("col")
    my_row = lax.axis_index("row")
    tok_all, width_loc = normed.shape
    tok_blk = tok_all // col_count
    head_column_span = projection_weight.shape[2]
    heads_loc = head_column_span // HEAD_DIM
    active_slots = slot_adapter_ids.shape[0]
    adapter_rank_width = adapter_up_weight.shape[2]
    prompt_starts = start_table(packed_prompt_length)
    slot_of = slot_table(prompt_adapter_ids, slot_adapter_ids)
    block_start = col_index * tok_blk
    mine = block_start + jnp.arange(tok_blk, dtype=jnp.int32)
    mine_prompts = token_prompts(mine, prompt_starts)
    mine_slots = token_slots(mine_prompts, slot_of)
    down_weight_slices = lax.all_to_all(
        adapter_down_weight, "col", split_axis=0, concat_axis=1, tiled=True
    )
    down_cols = down_weight_slices.reshape(width_loc, -1)
    own_rows = lax.all_to_all(normed, "col", split_axis=0, concat_axis=1, tiled=True)
    weight_piece = lax.all_gather(projection_weight, "col", axis=0, tiled=True)
    flat_piece = weight_piece.reshape(weight_piece.shape[0], -1)
    projection_total = jnp.dot(own_rows, flat_piece, preferred_element_type=jnp.float32)
    rows_per = tok_all // row_count
    row_first = my_row * rows_per
    row_positions = row_first + jnp.arange(rows_per, dtype=jnp.int32)
    row_slots = token_slots(token_prompts(row_positions, prompt_starts), slot_of)
    row_part = lax.dynamic_slice_in_dim(normed, row_first, rows_per, 0)
    summed = lax.psum(down_term(row_part, row_slots, down_cols, active_slots), "col")
    down_every = lax.all_gather(summed.astype(jnp.bfloat16), "row", axis=0, tiled=True)
    local_down_output = lax.dynamic_slice_in_dim(down_every, block_start, tok_blk, 0)
    pick_half = (mine_slots[:, None] == jnp.arange(active_slots, dtype=jnp.int32)[None, :]).astype(
        jnp.bfloat16
    )

    def reduced_rank_rows(low_part, slot_membership):
        token_spread = (pick_half[:, :, None] * low_part[:, None, :]).reshape(
            tok_blk, active_slots * adapter_rank_width
        )
        up_weight_table = adapter_up_weight[:, slot_membership].reshape(
            active_slots * adapter_rank_width, head_column_span
        )
        return jnp.dot(token_spread, up_weight_table, preferred_element_type=jnp.float32)

    query_token_rows = (
        projection_total[:, :head_column_span]
        + adapter_scale * reduced_rank_rows(local_down_output[:, :adapter_rank_width], 0)
    ).astype(jnp.bfloat16)
    key_rows = projection_total[:, head_column_span : 2 * head_column_span].astype(jnp.bfloat16)
    value_token_rows = (
        projection_total[:, 2 * head_column_span :]
        + adapter_scale * reduced_rank_rows(local_down_output[:, adapter_rank_width:], 1)
    ).astype(jnp.bfloat16)
    own_kv = jnp.stack([key_rows, value_token_rows], axis=1)
    earlier = [shifted(own_kv, "col", 1)]
    window = jnp.concatenate(earlier[::-1] + [own_kv], axis=0)
    window_len = window.shape[0]
    window_pos = block_start - NEAR * tok_blk + jnp.arange(window_len, dtype=jnp.int32)
    window_prompts = token_prompts(window_pos, prompt_starts)
    allowed = (mine_prompts[:, None] == window_prompts[None, :]) & (
        window_pos[None, :] <= mine[:, None]
    )
    query_heads = query_token_rows.reshape(tok_blk, heads_loc, HEAD_DIM)
    key_heads = window[:, 0].reshape(window_len, heads_loc, HEAD_DIM)
    value_heads = window[:, 1].reshape(window_len, heads_loc, HEAD_DIM)
    score_scale = HEAD_DIM ** (-0.5)
    scores = (
        jnp.einsum("qhd,khd->hqk", query_heads, key_heads, preferred_element_type=jnp.float32)
        * score_scale
    )
    limited = jnp.where(allowed[None], scores, masked_score)
    peak_score = jnp.max(limited, axis=2, keepdims=True)
    weight = jnp.where(allowed[None], jnp.exp(scores - peak_score), 0.0)
    denominator = jnp.sum(weight, axis=2)
    mixed_heads = jnp.einsum(
        "hqk,khd->qhd", weight.astype(jnp.bfloat16), value_heads, preferred_element_type=jnp.float32
    )
    attended = (
        (mixed_heads / jnp.transpose(denominator)[:, :, None])
        .reshape(tok_blk, head_column_span)
        .astype(jnp.bfloat16)
    )
    prev_kv = earlier[0]
    page_window = jnp.concatenate(
        [prev_kv, own_kv, jnp.zeros((PAGE, 2, head_column_span), jnp.bfloat16)], axis=0
    )
    max_pages = prompt_page_slots.shape[1]
    lens_rep = jnp.repeat(packed_prompt_length, max_pages)
    starts_rep = jnp.repeat(prompt_starts, max_pages)
    page_index = jnp.tile(jnp.arange(max_pages, dtype=jnp.int32), packed_prompt_length.shape[0])
    page_rows = jnp.clip(lens_rep - PAGE * page_index, 0, PAGE)
    page_first = starts_rep + PAGE * page_index
    my_slots = col_index * SLOTS_DEV + jnp.arange(SLOTS_DEV, dtype=jnp.int32)
    slot_hit = prompt_page_slots.reshape(-1)[None, :] == my_slots[:, None]
    rows_used = jnp.sum(jnp.where(slot_hit, page_rows[None, :], 0), axis=1)
    first_used = jnp.sum(jnp.where(slot_hit, page_first[None, :], 0), axis=1)
    offset = jnp.clip(first_used - (col_index - 1) * tok_blk, 0, 2 * tok_blk)
    page_lines = jnp.arange(PAGE, dtype=jnp.int32)
    pick_rows = (offset[:, None] + page_lines[None, :]).reshape(-1)
    taken_rows = jnp.take(page_window, pick_rows, axis=0).reshape(
        SLOTS_DEV, PAGE, 2, head_column_span
    )
    live_rows = (page_lines[None, :] < rows_used[:, None])[:, :, None, None]
    kv_pages = jnp.where(live_rows, taken_rows, jnp.zeros_like(taken_rows))
    return (attended, kv_pages)


def solution(mesh):
    placed = (
        P(None, "col"),
        P("col", None, "row"),
        P(None, "col", None),
        P(None, None, None, "row"),
        P(),
        P(),
        P(),
        P(),
    )
    return jax.shard_map(
        local,
        mesh=mesh,
        in_specs=placed,
        out_specs=(P("col", "row"), P("col", None, None, "row")),
        check_vma=False,
    )
```

profile of v0, /device:TPU:6, one launch (start us, length us, event | category | flops | bytes accessed | tf_op | source)
XLA Modules:
  0.0 544.9 jit_solution(5829252045479823222)
XLA Ops:
  8.4 1.9 reduce.3
  11.3 2.4 reshape.319
  13.7 7.4 %all-to-all-start.1 = ((bf16[16,2,7168]{2,1,0:T(2,128)(2,1)}), bf16[16,2,7168]{2,1,0:T(2,128)(2,1)S(1)}, u32[]{:S(2)}, u32[]{:S(2)}) async-start(bf16[16,2,7168]{2,1,0:T(2,128)(2,1)} %reshape.319), calls=%async_computation.1 | async-start | bytes 917504 | tf_op jit(solution)/shard_map/all_to_all | solution.py:77
  21.1 8.1 %copy.104 = bf16[56,16,8,512]{3,2,0,1:T(8,128)(2,1)} copy(bf16[56,16,8,512]{3,2,1,0:T(8,128)(2,1)} %bitcast.61) | data formatting | bytes 14680064 | tf_op jit(solution)/shard_map/all_to_all | solution.py:81
  29.2 1.7 all-to-all-done.1
  31.0 5.9 %all-to-all-start = ((bf16[16,512,448]{1,2,0:T(8,128)(2,1)}), bf16[16,512,448]{1,2,0:T(8,128)(2,1)}, u32[]{:S(2)}, u32[]{:S(2)}) async-start(bf16[16,512,448]{1,2,0:T(8,128)(2,1)} %bitcast.59), calls=%async_computation | async-start | bytes 14680064 | tf_op jit(solution)/shard_map/all_to_all | solution.py:81
  38.1 4.2 reshape.320
  42.4 7.0 %copy.84 = bf16[7168,1,32]{0,2,1:T(8,128)(2,1)S(1)} copy(bf16[7168,1,32]{2,1,0:T(2,128)(2,1)} %reshape.320) | data formatting | bytes 917504 | tf_op jit(solution)/shard_map/all_to_all | solution.py:77
  50.0 1.9 select_reduce_fusion.1
  52.0 199.3 %all-reduce.1 = bf16[1024,32]{0,1:T(8,128)(2,1)S(1)} all-reduce(f32[1024,32]{0,1:T(8,128)S(1)} %select_reduce_fusion.1), channel_id=1, replica_groups=mesh['row'=8,'col'=16] {'col'}, use_global_device_ids=true, to_apply=%region_7.8 | all-reduce | flops 32768 | bytes 196608 | tf_op jit(solution)/shard_map/psum | solution.py:90
  251.3 13.7 %all_gather.7 = bf16[8192,32]{0,1:T(8,128)(2,1)S(1)} all-gather(bf16[1024,32]{0,1:T(8,128)(2,1)S(1)} %all-reduce.1), channel_id=1, replica_groups=mesh['row'=8,'col'=16] {'row'}, dimensions={0}, use_global_device_ids=true | all-gather | bytes 589824 | tf_op jit(solution)/shard_map/all_gather | solution.py:91
  265.0 66.0 %all-gather.2.cloned.1.call-done = bf16[7168,3,896]{2,0,1:T(8,128)(2,1)} async-done(((bf16[448,3,896]{2,0,1:T(8,128)(2,1)}), bf16[7168,3,896]{2,0,1:T(8,128)(2,1)}) %all-gather.2.cloned.1.call-update) | async-done | bytes 38535184 | tf_op jit(solution)/shard_map/all_gather | solution.py:82
  331.0 51.4 %copy.81 = bf16[7168,3,896]{0,2,1:T(8,128)(2,1)} copy(bf16[7168,3,896]{2,0,1:T(8,128)(2,1)} %all-gather.2.cloned.1.call-done) | data formatting | bytes 77070336 | tf_op jit(solution)/shard_map/all_gather | solution.py:82
  382.4 28.4 %fusion.38 = f32[512,2688]{1,0:T(8,128)} fusion(bf16[512,7168]{0,1:T(8,128)(2,1)} %bitcast.1, bf16[7168,2688]{0,1:T(8,128)(2,1)} %bitcast.58), kind=kOutput, calls=%fused_computation.78 | convolution fusion | flops 19730006016 | bytes 51380224 | tf_op jit(solution)/shard_map/dot_general | solution.py:84
  410.8 1.6 fusion.16
  412.4 2.0 fusion.15
  414.3 1.4 pad_maximum_fusion
  415.8 1.9 collective-permute-start
  418.6 1.3 compare_and_fusion
  419.9 2.0 fusion.10
  421.9 1.5 copy.87
  423.4 41.3 %collective-permute-done = bf16[512,2,896]{2,0,1:T(8,128)(2,1)} collective-permute-done((bf16[512,2,896]{2,0,1:T(8,128)(2,1)}, bf16[512,2,896]{2,0,1:T(8,128)(2,1)}, u32[]{:S(2)}, u32[]{:S(2)}) %collective-permute-start) | collective-permute-done | bytes 1835040 | tf_op jit(solution)/shard_map/ppermute | solution.py:17
  464.7 1.8 maximum_maximum_fusion.1
  466.5 2.1 fusion.35
  468.6 3.8 copy.88
  472.5 3.1 maximum_maximum_fusion
  475.7 15.3 %copy.92 = bf16[1152,2,896]{2,1,0:T(2,128)(2,1)} copy(bf16[1152,2,896]{2,0,1:T(8,128)(2,1)S(1)} %maximum_maximum_fusion) | data formatting | bytes 8257536 | tf_op jit(solution)/shard_map/concatenate | solution.py:145
  490.9 2.4 copy.86
  493.3 12.7 %fusion.37 = (f32[7,512]{1,0:T(8,128)S(1)}, bf16[7,512,1024]{2,1,0:T(8,128)(2,1)}) fusion(pred[512,1024]{1,0:T(8,128)(4,1)S(1)} %copy-done.4, bf16[512,7,128]{0,2,1:T(8,128)(2,1)S(1)} %bitcast.68, bf16[1024,7,128]{0,2,1:T(8,128)(2,1)} %bitcast.62), kind=kOutput, calls=%fused_computation.77 | convolution fusion | flops 1904739328 | bytes 10631168 | tf_op jit(solution)/shard_map/sub | solution.py:134
  506.0 5.7 %fusion.12 = bf16[512,7,128]{0,2,1:T(8,128)(2,1)S(1)} fusion(bf16[1024,7,128]{0,2,1:T(8,128)(2,1)S(1)} %bitcast.63, bf16[7,512,1024]{2,1,0:T(8,128)(2,1)} %get-tuple-element.29, f32[512,7]{0,1:T(8,128)S(1)} %bitcast.72), kind=kOutput, calls=%fused_computation.25 | convolution fusion | flops 940441600 | bytes 10106880 | tf_op jit(solution)/shard_map/hqk,khd->qhd/dot_general | solution.py:136
  513.0 16.6 %gather_fusion = bf16[1280,2,896]{2,1,0:T(2,128)(2,1)} fusion(bf16[1152,2,896]{2,1,0:T(2,128)(2,1)} %copy.92, s32[2048]{0:T(1024)S(1)} %pad_clamp_fusion), kind=kCustom, calls=%fused_computation | custom fusion | bytes 9180160 | tf_op jit(solution)/shard_map/jit(_take)/gather | solution.py:161
  529.6 8.5 %broadcast_select_fusion.1 = bf16[10,128,2,896]{3,2,1,0:T(2,128)(2,1)} fusion(pred[10,128]{1,0:T(8,128)(4,1)S(1)} %iota_compare_fusion.4, bf16[10,128,2,896]{3,2,1,0:T(2,128)(2,1)} %bitcast.60, pred[10,128]{1,0:T(8,128)(4,1)S(1)} %fusion.28), kind=kLoop, calls=%fused_computation.7 | loop fusion | flops 4587520 | bytes 9177600 | tf_op jit(solution)/shard_map/jit(_where)/select_n | solution.py:165
  (60 shorter events, 6.1 us)
Async XLA Ops:
  7.2 323.8 %all-gather.2.cloned.1.call-start = ((), (), s32[]{:S(2)}) async-start(), calls=%async_computation.2 | async-start | bytes 40943616 | tf_op jit(solution)/shard_map/all_gather | solution.py:82
  13.7 17.3 %all-to-all-start.1 = ((bf16[16,2,7168]{2,1,0:T(2,128)(2,1)}), bf16[16,2,7168]{2,1,0:T(2,128)(2,1)S(1)}, u32[]{:S(2)}, u32[]{:S(2)}) async-start(bf16[16,2,7168]{2,1,0:T(2,128)(2,1)} %reshape.319), calls=%async_computation.1 | async-start | bytes 917504 | tf_op jit(solution)/shard_map/all_to_all | solution.py:77
  31.0 5.9 %copy-start.5 = (s32[64]{0:T(128)S(1)}, s32[64]{0:T(128)}, u32[]{:S(2)}) copy-start(s32[64]{0:T(128)} %param.12) | copy-start | bytes 772
  31.0 6.3 %copy-start.7 = (s32[64]{0:T(128)S(1)}, s32[64]{0:T(128)}, u32[]{:S(2)}) copy-start(s32[64]{0:T(128)} %param.13) | copy-start | bytes 772
  31.0 6.3 %copy-start.8 = (s32[16]{0:T(128)S(1)}, s32[16]{0:T(128)}, u32[]{:S(2)}) copy-start(s32[16]{0:T(128)} %param.14) | copy-start | bytes 196
  31.0 7.1 %copy-start.2 = (bf16[16,2,16,896]{3,2,1,0:T(8,128)(2,1)S(1)}, bf16[16,2,16,896]{3,2,1,0:T(8,128)(2,1)}, u32[]{:S(2)}) copy-start(bf16[16,2,16,896]{3,2,1,0:T(8,128)(2,1)} %param.11) | copy-start | bytes 2752516
  31.0 351.4 %all-to-all-start = ((bf16[16,512,448]{1,2,0:T(8,128)(2,1)}), bf16[16,512,448]{1,2,0:T(8,128)(2,1)}, u32[]{:S(2)}, u32[]{:S(2)}) async-start(bf16[16,512,448]{1,2,0:T(8,128)(2,1)} %bitcast.59), calls=%async_computation | async-start | bytes 14680064 | tf_op jit(solution)/shard_map/all_to_all | solution.py:81
  410.8 6.9 %copy-start.6 = (s32[64,4]{0,1:T(4,128)S(1)}, s32[64,4]{0,1:T(4,128)}, u32[]{:S(2)}) copy-start(s32[64,4]{0,1:T(4,128)} %param.15) | copy-start | bytes 3076
  415.8 49.0 %collective-permute-start = (bf16[512,2,896]{2,0,1:T(8,128)(2,1)}, bf16[512,2,896]{2,0,1:T(8,128)(2,1)}, u32[]{:S(2)}, u32[]{:S(2)}) collective-permute-start(bf16[512,2,896]{2,0,1:T(8,128)(2,1)} %pad_maximum_fusion), channel_id=1, source_target_pairs={{0,1},{1,2},{2,3},{3,4},{4,5},{5,6},{6,7},{7,8},{8,9},{9,10},{10,1... | collective-permute-start | bytes 5505032 | tf_op jit(solution)/shard_map/ppermute | solution.py:17
  475.6 15.3 %copy-start = (bf16[1024,1,896]{2,0,1:T(8,128)(2,1)S(1)}, bf16[1024,1,896]{2,0,1:T(8,128)(2,1)}, u32[]{:S(2)}) copy-start(bf16[1024,1,896]{2,0,1:T(8,128)(2,1)} %get-tuple-element.21) | copy-start | bytes 5505028
  475.6 17.7 %copy-start.3 = (bf16[512,896]{0,1:T(8,128)(2,1)S(1)}, bf16[512,896]{0,1:T(8,128)(2,1)}, u32[]{:S(2)}) copy-start(bf16[512,896]{0,1:T(8,128)(2,1)} %copy.87) | copy-start | bytes 2752516
  475.6 17.7 %copy-start.4 = (pred[512,1024]{1,0:T(8,128)(4,1)S(1)}, pred[512,1024]{1,0:T(8,128)(4,1)}, u32[]{:S(2)}) copy-start(pred[512,1024]{1,0:T(8,128)(4,1)} %compare_and_fusion) | copy-start | bytes 1572868
  493.3 12.7 %copy-start.1 = (bf16[1024,1,896]{0,2,1:T(8,128)(2,1)S(1)}, bf16[1024,1,896]{0,2,1:T(8,128)(2,1)}, u32[]{:S(2)}) copy-start(bf16[1024,1,896]{0,2,1:T(8,128)(2,1)} %copy.86) | copy-start | bytes 5505028
Sparse Core Ops, SparseCore 0:
  10.1 320.8 all-gather.1
where the time goes:
time: 547 us; the launch traced here: 545 us
  blocking collectives  213 us (39%)
  local copies, waits for them, and re-layouts  120 us (22%)
  waiting for transfers between devices  110 us (20%)
  matrix products  52.6 us (10%)
  other arithmetic  19.5 us (4%)
  starting transfers between devices  15.3 us (3%)
  between operations  14.3 us (3%)
    psum x1, blocking collectives, local(): lax.psum(down_term(row_part, row_slots, down_cols, active_slots), 'col')  199 us
    all_gather x1, waiting for transfers between devices, local(): weight_piece = lax.all_gather(projection_weight, 'col', axis=0, tiled=True)  66 us
    all_gather x1, local copies, waits for them, and re-layouts, local(): weight_piece = lax.all_gather(projection_weight, 'col', axis=0, tiled=True)  51.4 us
    ppermute x1, waiting for transfers between devices, shifted(): return lax.ppermute(block, axis, route)  41.3 us
    dot_general x1, matrix products, local(): jnp.dot(own_rows, flat_piece, preferred_element_type=jnp.float32)  28.4 us
    gather x1, local copies, waits for them, and re-layouts, local(): jnp.take(page_window, pick_rows, axis=0)  16.6 us
    concatenate x2, local copies, waits for them, and re-layouts, local(): jnp.concatenate([prev_kv, own_kv, jnp.zeros((PAGE, 2, head_column_span),...  15.3 us
    all_gather x1, blocking collectives, local(): lax.all_gather(summed.astype(jnp.bfloat16), 'row', axis=0, tiled=True)  13.7 us
  transfers between devices with their start and end apart: 4, of which 3 were waited for; matrix products, arithmetic and copies ran while one was open for 16% of the time, Pallas kernels for 0%

commit v1 on v0

--- a/solution.py
+++ b/solution.py
@@ -9,6 +9,27 @@
 SLOTS_DEV = 10
 adapter_scale = 2.0
 masked_score = -1e30
+
+
+def ring_gather(value, axis, dim):
+    devices, position, rows = (lax.axis_size(axis), lax.axis_index(axis), value.shape[dim])
+    right = [(i, (i + 1) % devices) for i in range(devices)]
+    left = [(i, (i - 1) % devices) for i in range(devices)]
+    out = jnp.zeros((*value.shape[:dim], devices * rows, *value.shape[dim + 1 :]), value.dtype)
+    out = lax.dynamic_update_slice_in_dim(out, value, position * rows, axis=dim)
+    from_left = from_right = value
+    half = devices // 2
+    for lap in range(1, half + 1):
+        from_left = lax.ppermute(from_left, axis, right)
+        out = lax.dynamic_update_slice_in_dim(
+            out, from_left, (position - lap) % devices * rows, axis=dim
+        )
+        if lap < devices - half:
+            from_right = lax.ppermute(from_right, axis, left)
+            out = lax.dynamic_update_slice_in_dim(
+                out, from_right, (position + lap) % devices * rows, axis=dim
+            )
+    return out
 
 
 def shifted(block, axis, distance):
@@ -88,7 +109,7 @@
     row_slots = token_slots(token_prompts(row_positions, prompt_starts), slot_of)
     row_part = lax.dynamic_slice_in_dim(normed, row_first, rows_per, 0)
     summed = lax.psum(down_term(row_part, row_slots, down_cols, active_slots), "col")
-    down_every = lax.all_gather(summed.astype(jnp.bfloat16), "row", axis=0, tiled=True)
+    down_every = ring_gather(summed.astype(jnp.bfloat16), "row", 0)
     local_down_output = lax.dynamic_slice_in_dim(down_every, block_start, tok_blk, 0)
     pick_half = (mine_slots[:, None] == jnp.arange(active_slots, dtype=jnp.int32)[None, :]).astype(
         jnp.bfloat16

time: 547 us -> 547 us (level)
  blocking collectives: 213 us -> 199 us
  starting transfers between devices: 15.3 us -> 25.2 us
    all_gather x1 -> x0, blocking collectives: 13.7 us -> none  [local(): lax.all_gather(summed.astype(jnp.bfloat16), 'row', axis=0, tiled=True)]
    ppermute x0 -> x7, waiting for transfers between devices: none -> 9.74 us  [the longest x4 8.64 us: ring_gather(): from_left = lax.ppermute(from_left, axis, right)]
    ppermute x0 -> x7, starting transfers between devices: none -> 9.71 us  [the longest x3 9.69 us: ring_gather(): from_right = lax.ppermute(from_right, axis, left)]
    all_gather x1, waiting for transfers between devices: 66 us -> 60 us  [local(): weight_piece = lax.all_gather(projection_weight, 'col', axis=0, tiled=True)]
  transfers between devices with their start and end apart: 4 -> 11, of which waited for: 3 -> 9; matrix products, arithmetic and copies ran while one was open for 16% -> 16% of each run, Pallas kernels for 0% -> 0%
where the time goes in v1:
time: 547 us; the launch traced here: 545 us
  blocking collectives  199 us (36%)
  local copies, waits for them, and re-layouts  120 us (22%)
  waiting for transfers between devices  114 us (21%)
  matrix products  52.6 us (10%)
  starting transfers between devices  25.2 us (5%)
  other arithmetic  19.5 us (4%)
  between operations  14.4 us (3%)
    psum x1, blocking collectives, local(): lax.psum(down_term(row_part, row_slots, down_cols, active_slots), 'col')  199 us
    all_gather x1, waiting for transfers between devices, local(): weight_piece = lax.all_gather(projection_weight, 'col', axis=0, tiled=True)  60 us
    all_gather x1, local copies, waits for them, and re-layouts, local(): weight_piece = lax.all_gather(projection_weight, 'col', axis=0, tiled=True)  51.4 us
    ppermute x1, waiting for transfers between devices, shifted(): return lax.ppermute(block, axis, route)  41.4 us
    dot_general x1, matrix products, local(): jnp.dot(own_rows, flat_piece, preferred_element_type=jnp.float32)  28.4 us
    gather x1, local copies, waits for them, and re-layouts, local(): jnp.take(page_window, pick_rows, axis=0)  16.5 us
    concatenate x2, local copies, waits for them, and re-layouts, local(): jnp.concatenate([prev_kv, own_kv, jnp.zeros((PAGE, 2, head_column_span),...  15.3 us
    sub x1, matrix products, local(): weight = jnp.where(allowed[None], jnp.exp(scores - peak_score), 0.0)  12.7 us
  transfers between devices with their start and end apart: 11, of which 9 were waited for; matrix products, arithmetic and copies ran while one was open for 16% of the time, Pallas kernels for 0%

profile of v1, /device:TPU:6, one launch (start us, length us, event | category | flops | bytes accessed | tf_op | source)
XLA Modules:
  0.0 544.8 jit_solution(1952589002538246852)
XLA Ops:
  8.4 1.9 reduce.3
  11.3 2.4 reshape.319
  13.7 7.4 %all-to-all-start.1 = ((bf16[16,2,7168]{2,1,0:T(2,128)(2,1)}), bf16[16,2,7168]{2,1,0:T(2,128)(2,1)S(1)}, u32[]{:S(2)}, u32[]{:S(2)}) async-start(bf16[16,2,7168]{2,1,0:T(2,128)(2,1)} %reshape.319), calls=%async_computation.1 | async-start | bytes 917504 | tf_op jit(solution)/shard_map/all_to_all | solution.py:98
  21.1 8.1 %copy.104 = bf16[56,16,8,512]{3,2,0,1:T(8,128)(2,1)} copy(bf16[56,16,8,512]{3,2,1,0:T(8,128)(2,1)} %bitcast.61) | data formatting | bytes 14680064 | tf_op jit(solution)/shard_map/all_to_all | solution.py:102
  29.2 1.7 all-to-all-done.1
  31.0 5.9 %all-to-all-start = ((bf16[16,512,448]{1,2,0:T(8,128)(2,1)}), bf16[16,512,448]{1,2,0:T(8,128)(2,1)}, u32[]{:S(2)}, u32[]{:S(2)}) async-start(bf16[16,512,448]{1,2,0:T(8,128)(2,1)} %bitcast.59), calls=%async_computation | async-start | bytes 14680064 | tf_op jit(solution)/shard_map/all_to_all | solution.py:102
  38.2 4.2 reshape.320
  42.4 7.0 %copy.84 = bf16[7168,1,32]{0,2,1:T(8,128)(2,1)S(1)} copy(bf16[7168,1,32]{2,1,0:T(2,128)(2,1)} %reshape.320) | data formatting | bytes 917504 | tf_op jit(solution)/shard_map/all_to_all | solution.py:98
  50.1 1.9 select_reduce_fusion.1
  52.0 199.3 %all-reduce.1 = bf16[1024,32]{0,1:T(8,128)(2,1)S(1)} all-reduce(f32[1024,32]{0,1:T(8,128)S(1)} %select_reduce_fusion.1), channel_id=1, replica_groups=mesh['row'=8,'col'=16] {'col'}, use_global_device_ids=true, to_apply=%region_7.8 | all-reduce | flops 32768 | bytes 196608 | tf_op jit(solution)/shard_map/psum | solution.py:111
  251.3 2.9 collective-permute-start.1
  254.3 1.9 collective-permute-done
  256.2 3.4 collective-permute-start.3
  261.4 3.4 collective-permute-start.5
  266.8 4.1 collective-permute-done.6
  271.0 60.0 %all-gather.2.cloned.1.call-done = bf16[7168,3,896]{2,0,1:T(8,128)(2,1)} async-done(((bf16[448,3,896]{2,0,1:T(8,128)(2,1)}), bf16[7168,3,896]{2,0,1:T(8,128)(2,1)}) %all-gather.2.cloned.1.call-update) | async-done | bytes 38535184 | tf_op jit(solution)/shard_map/all_gather | solution.py:103
  331.0 51.4 %copy.81 = bf16[7168,3,896]{0,2,1:T(8,128)(2,1)} copy(bf16[7168,3,896]{2,0,1:T(8,128)(2,1)} %all-gather.2.cloned.1.call-done) | data formatting | bytes 77070336 | tf_op jit(solution)/shard_map/all_gather | solution.py:103
  382.4 28.4 %fusion.38 = f32[512,2688]{1,0:T(8,128)} fusion(bf16[512,7168]{0,1:T(8,128)(2,1)} %bitcast.1, bf16[7168,2688]{0,1:T(8,128)(2,1)} %bitcast.58), kind=kOutput, calls=%fused_computation.86 | convolution fusion | flops 19730006016 | bytes 51380224 | tf_op jit(solution)/shard_map/dot_general | solution.py:105
  412.4 2.0 fusion.15
  415.8 2.1 collective-permute-start.7
  420.1 2.0 fusion.10
  423.3 41.4 %collective-permute-done.7 = bf16[512,2,896]{2,0,1:T(8,128)(2,1)} collective-permute-done((bf16[512,2,896]{2,0,1:T(8,128)(2,1)}, bf16[512,2,896]{2,0,1:T(8,128)(2,1)}, u32[]{:S(2)}, u32[]{:S(2)}) %collective-permute-start.7) | collective-permute-done | bytes 1835040 | tf_op jit(solution)/shard_map/ppermute | solution.py:38
  464.7 1.8 maximum_maximum_fusion.1
  466.5 2.1 fusion.35
  468.6 3.8 copy.88
  472.5 3.1 maximum_maximum_fusion
  475.7 15.3 %copy.92 = bf16[1152,2,896]{2,1,0:T(2,128)(2,1)} copy(bf16[1152,2,896]{2,0,1:T(8,128)(2,1)S(1)} %maximum_maximum_fusion) | data formatting | bytes 8257536 | tf_op jit(solution)/shard_map/concatenate | solution.py:166
  490.9 2.4 copy.86
  493.3 12.7 %fusion.37 = (f32[7,512]{1,0:T(8,128)S(1)}, bf16[7,512,1024]{2,1,0:T(8,128)(2,1)}) fusion(pred[512,1024]{1,0:T(8,128)(4,1)S(1)} %copy-done.4, bf16[512,7,128]{0,2,1:T(8,128)(2,1)S(1)} %bitcast.68, bf16[1024,7,128]{0,2,1:T(8,128)(2,1)} %bitcast.62), kind=kOutput, calls=%fused_computation.85 | convolution fusion | flops 1904739328 | bytes 10631168 | tf_op jit(solution)/shard_map/sub | solution.py:155
  506.0 5.7 %fusion.12 = bf16[512,7,128]{0,2,1:T(8,128)(2,1)S(1)} fusion(bf16[1024,7,128]{0,2,1:T(8,128)(2,1)S(1)} %bitcast.63, bf16[7,512,1024]{2,1,0:T(8,128)(2,1)} %get-tuple-element.29, f32[512,7]{0,1:T(8,128)S(1)} %bitcast.72), kind=kOutput, calls=%fused_computation.25 | convolution fusion | flops 940441600 | bytes 10106880 | tf_op jit(solution)/shard_map/hqk,khd->qhd/dot_general | solution.py:157
  513.0 16.5 %gather_fusion = bf16[1280,2,896]{2,1,0:T(2,128)(2,1)} fusion(bf16[1152,2,896]{2,1,0:T(2,128)(2,1)} %copy.92, s32[2048]{0:T(1024)S(1)} %pad_clamp_fusion), kind=kCustom, calls=%fused_computation | custom fusion | bytes 9180160 | tf_op jit(solution)/shard_map/jit(_take)/gather | solution.py:182
  529.5 8.5 %broadcast_select_fusion.1 = bf16[10,128,2,896]{3,2,1,0:T(2,128)(2,1)} fusion(pred[10,128]{1,0:T(8,128)(4,1)S(1)} %iota_compare_fusion.4, bf16[10,128,2,896]{3,2,1,0:T(2,128)(2,1)} %bitcast.60, pred[10,128]{1,0:T(8,128)(4,1)S(1)} %fusion.28), kind=kLoop, calls=%fused_computation.7 | loop fusion | flops 4587520 | bytes 9177600 | tf_op jit(solution)/shard_map/jit(_where)/select_n | solution.py:186
  (82 shorter events, 15.6 us)
Async XLA Ops:
  7.2 323.8 %all-gather.2.cloned.1.call-start = ((), (), s32[]{:S(2)}) async-start(), calls=%async_computation.2 | async-start | bytes 40943616 | tf_op jit(solution)/shard_map/all_gather | solution.py:103
  13.7 17.3 %all-to-all-start.1 = ((bf16[16,2,7168]{2,1,0:T(2,128)(2,1)}), bf16[16,2,7168]{2,1,0:T(2,128)(2,1)S(1)}, u32[]{:S(2)}, u32[]{:S(2)}) async-start(bf16[16,2,7168]{2,1,0:T(2,128)(2,1)} %reshape.319), calls=%async_computation.1 | async-start | bytes 917504 | tf_op jit(solution)/shard_map/all_to_all | solution.py:98
  31.0 5.9 %copy-start.5 = (s32[64]{0:T(128)S(1)}, s32[64]{0:T(128)}, u32[]{:S(2)}) copy-start(s32[64]{0:T(128)} %param.12) | copy-start | bytes 772
  31.0 6.3 %copy-start.7 = (s32[64]{0:T(128)S(1)}, s32[64]{0:T(128)}, u32[]{:S(2)}) copy-start(s32[64]{0:T(128)} %param.13) | copy-start | bytes 772
  31.0 6.3 %copy-start.8 = (s32[16]{0:T(128)S(1)}, s32[16]{0:T(128)}, u32[]{:S(2)}) copy-start(s32[16]{0:T(128)} %param.14) | copy-start | bytes 196
  31.0 7.1 %copy-start.2 = (bf16[16,2,16,896]{3,2,1,0:T(8,128)(2,1)S(1)}, bf16[16,2,16,896]{3,2,1,0:T(8,128)(2,1)}, u32[]{:S(2)}) copy-start(bf16[16,2,16,896]{3,2,1,0:T(8,128)(2,1)} %param.11) | copy-start | bytes 2752516
  31.0 351.4 %all-to-all-start = ((bf16[16,512,448]{1,2,0:T(8,128)(2,1)}), bf16[16,512,448]{1,2,0:T(8,128)(2,1)}, u32[]{:S(2)}, u32[]{:S(2)}) async-start(bf16[16,512,448]{1,2,0:T(8,128)(2,1)} %bitcast.59), calls=%async_computation | async-start | bytes 14680064 | tf_op jit(solution)/shard_map/all_to_all | solution.py:102
  251.3 4.9 collective-permute-start
  251.3 4.9 collective-permute-start.1
  256.2 4.9 collective-permute-start.2
  256.2 5.3 collective-permute-start.3
  261.1 4.9 collective-permute-start.4
  261.4 5.3 collective-permute-start.5
  266.0 4.9 collective-permute-start.6
  410.8 7.1 %copy-start.6 = (s32[64,4]{0,1:T(4,128)S(1)}, s32[64,4]{0,1:T(4,128)}, u32[]{:S(2)}) copy-start(s32[64,4]{0,1:T(4,128)} %param.15) | copy-start | bytes 3076
  415.8 49.0 %collective-permute-start.7 = (bf16[512,2,896]{2,0,1:T(8,128)(2,1)}, bf16[512,2,896]{2,0,1:T(8,128)(2,1)}, u32[]{:S(2)}, u32[]{:S(2)}) collective-permute-start(bf16[512,2,896]{2,0,1:T(8,128)(2,1)} %pad_maximum_fusion), channel_id=1, source_target_pairs={{0,1},{1,2},{2,3},{3,4},{4,5},{5,6},{6,7},{7,8},{8,9},{9,10},{10,1... | collective-permute-start | bytes 5505032 | tf_op jit(solution)/shard_map/ppermute | solution.py:38
  475.6 15.3 %copy-start = (bf16[1024,1,896]{2,0,1:T(8,128)(2,1)S(1)}, bf16[1024,1,896]{2,0,1:T(8,128)(2,1)}, u32[]{:S(2)}) copy-start(bf16[1024,1,896]{2,0,1:T(8,128)(2,1)} %get-tuple-element.21) | copy-start | bytes 5505028
  475.6 17.7 %copy-start.3 = (bf16[512,896]{0,1:T(8,128)(2,1)S(1)}, bf16[512,896]{0,1:T(8,128)(2,1)}, u32[]{:S(2)}) copy-start(bf16[512,896]{0,1:T(8,128)(2,1)} %copy.87) | copy-start | bytes 2752516
  475.6 17.7 %copy-start.4 = (pred[512,1024]{1,0:T(8,128)(4,1)S(1)}, pred[512,1024]{1,0:T(8,128)(4,1)}, u32[]{:S(2)}) copy-start(pred[512,1024]{1,0:T(8,128)(4,1)} %compare_and_fusion) | copy-start | bytes 1572868
  493.3 12.7 %copy-start.1 = (bf16[1024,1,896]{0,2,1:T(8,128)(2,1)S(1)}, bf16[1024,1,896]{0,2,1:T(8,128)(2,1)}, u32[]{:S(2)}) copy-start(bf16[1024,1,896]{0,2,1:T(8,128)(2,1)} %copy.86) | copy-start | bytes 5505028
Sparse Core Ops, SparseCore 0:
  10.1 320.8 all-gather.1
